TPU v7x, 1024 devices: a whole 4x4x32 slice. The times are simulated.
1024 devices in a mesh: grp: 16 (over x, y_hi, core), qb: 64 (over z, y_lo).
Axes of the slice: x: 4, y: 4 (y_hi: 2, y_lo: 2; y = y_hi * 2 + y_lo), z: 32, core: 2. Of those that a mesh axis runs over, the one named last changes fastest.
Arguments:
- amplitudes: float32 [2, 134217728], P(None, ('grp', 'qb')), may hold values from -6 to 6
- layer_gates: float32 [4, 2, 128, 128], replicated, may hold values from -0.375 to 0.375
- cross_gates: float32 [2, 2, 4, 4], replicated, may hold values from -2 to 2
Outputs:
- final_state: float32 [2, 134217728], P(None, ('grp', 'qb'))
All inputs are finite; a program needn't handle non-finite values.
Results may differ from a plain program's by a relative error of at most 0.000084.
Values sent between devices are 32-bit elements; how exact they have to be, the bound alone decides.
A program may use at most 32 MiB of HBM per device.

v0:
```python
import jax
import jax.numpy as jnp
from jax import lax
from jax.sharding import PartitionSpec as P


def from_partner(value, axis, distance):
    mask = 2**distance
    pairs = [(source, source ^ mask) for source in range(lax.axis_size(axis))]
    return lax.ppermute(value, axis, pairs)


def dot_parts(first, second, numbers):

    def product(left, right):
        return lax.dot_general(
            left,
            right,
            numbers,
            precision=lax.Precision.HIGHEST,
            preferred_element_type=jnp.float32,
        )

    real_part = product(first[0], second[0]) - product(first[1], second[1])
    imag_part = product(first[0], second[1]) + product(first[1], second[0])
    return jnp.stack([real_part, imag_part])


def apply_high(amplitudes, matrix):
    width = matrix.shape[-1]
    blocks = amplitudes.reshape(2, width, -1)
    return dot_parts(matrix, blocks, (((1,), (0,)), ((), ()))).reshape(2, -1)


def apply_low(amplitudes, matrix):
    width = matrix.shape[-1]
    blocks = amplitudes.reshape(2, -1, width)
    return dot_parts(blocks, matrix, (((1,), (1,)), ((), ()))).reshape(2, -1)


def pick_coefficient(matrix, row_index, col_index):
    counter = jnp.arange(4, dtype=jnp.int32)
    chosen = (counter[:, None] == row_index) & (counter[None, :] == col_index)
    return jnp.sum(jnp.where(chosen[None], matrix, 0.0), axis=(1, 2))


def partner(amplitudes, position):
    return from_partner(amplitudes, "grp", position)


def pair_gate(amplitudes, matrix, lowest):
    own_bits = lax.axis_index("grp") // 2**lowest % 4
    first = partner(amplitudes, lowest)
    second = partner(amplitudes, lowest + 1)
    third = partner(first, lowest + 1)
    real_total = jnp.zeros_like(amplitudes[0])
    imag_total = jnp.zeros_like(amplitudes[0])
    for offset, source in enumerate((amplitudes, first, second, third)):
        weight = pick_coefficient(matrix, own_bits, jnp.bitwise_xor(own_bits, offset))
        real_total = real_total + weight[0] * source[0] - weight[1] * source[1]
        imag_total = imag_total + weight[0] * source[1] + weight[1] * source[0]
    return jnp.stack([real_total, imag_total])


def on_device(amplitudes, layer_gates, cross_gates):
    section_one = apply_high(amplitudes, layer_gates[0])
    section_two = apply_low(section_one, layer_gates[1])
    inner = lax.axis_size("qb")
    blocks = section_two.reshape(2, inner, -1)
    swapped = lax.all_to_all(blocks, "qb", split_axis=1, concat_axis=1, tiled=True).reshape(2, -1)
    section_three = apply_high(swapped, layer_gates[2])
    section_four = apply_low(section_three, layer_gates[3])
    groups = lax.axis_size("grp")
    top_bits = groups.bit_length() - 1
    section_five = pair_gate(section_four, cross_gates[0], 0)
    final_state = pair_gate(section_five, cross_gates[1], top_bits - 2)
    return final_state


def solution(mesh):
    return jax.shard_map(
        on_device,
        mesh=mesh,
        in_specs=(P(None, ("grp", "qb")), P(), P()),
        out_specs=P(None, ("grp", "qb")),
        check_vma=False,
    )
```

profile of v0, /device:TPU:24, one launch (start us, length us, event | category | flops | bytes accessed | tf_op | source)
XLA Modules:
  0.0 323.7 jit_solution(153377377312301837)
XLA Ops:
  0.0 4.4 %slice_reduce_fusion.2 = (f32[131072]{0:T(1024)S(1)}, f32[131072]{0:T(1024)S(1)}) fusion(f32[2,131072]{1,0:T(2,128)} %param.3), kind=kLoop, calls=%fused_computation.20 | loop fusion | bytes 2097152 | tf_op jit(solution)/shard_map/slice | solution.py:24
  4.6 0.9 copy-done
  10.5 0.9 pad_maximum_fusion
  11.4 139.9 %all_to_all.5 = f32[2,64,2048]{2,0,1:T(2,128)S(1)} all-to-all(f32[2,64,2048]{2,0,1:T(2,128)S(1)} %pad_maximum_fusion), channel_id=1, replica_groups=mesh['grp'=16,'qb'=64] {'qb'}, dimensions={1} | all-to-all | bytes 2097152 | tf_op jit(solution)/shard_map/all_to_all | solution.py:70
  151.3 2.7 slice_reduce_fusion
  154.2 1.0 fusion.12
  155.2 1.0 fusion.10
  156.2 1.0 fusion.1
  158.7 1.0 fusion
  161.2 0.9 pad_maximum_fusion.1
  162.1 1.9 collective-permute-start
  164.1 3.1 collective-permute-start.1
  167.3 4.4 %collective-permute-start.2 = (f32[2,131072]{1,0:T(2,128)S(1)}, f32[2,131072]{1,0:T(2,128)S(1)}, u32[]{:S(2)}, u32[]{:S(2)}) collective-permute-start(f32[2,131072]{1,0:T(2,128)S(1)} %collective-permute-done), channel_id=1, source_target_pairs={{0,128},{64,192},{128,0},{192,64},{256,384},{320,448},{384,256},{4... | collective-permute-start | bytes 3145736 | tf_op jit(solution)/shard_map/ppermute | solution.py:10
  171.9 0.7 copy-done.1
  172.7 0.7 fusion.57
  174.0 0.6 fusion.55
  175.2 18.4 %collective-permute-done.1 = f32[2,131072]{1,0:T(2,128)S(1)} collective-permute-done((f32[2,131072]{1,0:T(2,128)S(1)}, f32[2,131072]{1,0:T(2,128)S(1)}, u32[]{:S(2)}, u32[]{:S(2)}) %collective-permute-start.1) | collective-permute-done | bytes 1048608 | tf_op jit(solution)/shard_map/ppermute | solution.py:10
  193.6 22.0 %collective-permute-done.2 = f32[2,131072]{1,0:T(2,128)S(1)} collective-permute-done((f32[2,131072]{1,0:T(2,128)S(1)}, f32[2,131072]{1,0:T(2,128)S(1)}, u32[]{:S(2)}, u32[]{:S(2)}) %collective-permute-start.2) | collective-permute-done | bytes 1048608 | tf_op jit(solution)/shard_map/ppermute | solution.py:10
  215.6 7.9 %multiply_subtract_fusion.1 = f32[1,131072]{1,0:T(1,128)S(1)} fusion(f32[1,131072]{1,0:T(1,128)S(1)} %bitcast.110, f32[1,131072]{1,0:T(1,128)S(1)} %bitcast.107, f32[2,131072]{1,0:T(2,128)S(1)} %collective-permute-done.2, f32[2,131072]{1,0:T(2,128)S(1)} %collective-permute-done.1, f32[2,131072]{1,0:T(2,128)S(1)} %collective-permute-done, f32[]{:T(128)} %bitcast.24, ...), kind=kLoop, calls=%fused_computation.19 | loop fusion | flops 1966080 | bytes 4718624 | tf_op jit(solution)/shard_map/sub | solution.py:60
  223.4 7.9 %multiply_add_fusion.1 = f32[1,131072]{1,0:T(1,128)S(1)} fusion(f32[1,131072]{1,0:T(1,128)S(1)} %bitcast.108, f32[1,131072]{1,0:T(1,128)S(1)} %bitcast.111, f32[2,131072]{1,0:T(2,128)S(1)} %collective-permute-done.2, f32[2,131072]{1,0:T(2,128)S(1)} %collective-permute-done.1, f32[2,131072]{1,0:T(2,128)S(1)} %collective-permute-done, f32[]{:T(128)} %bitcast.24, ...), kind=kLoop, calls=%fused_computation.18 | loop fusion | flops 1966080 | bytes 4718624 | tf_op jit(solution)/shard_map/add | solution.py:61
  231.3 0.9 pad_maximum_fusion.2
  232.3 3.4 %collective-permute-start.3 = (f32[2,131072]{1,0:T(2,128)S(1)}, f32[2,131072]{1,0:T(2,128)S(1)}, u32[]{:S(2)}, u32[]{:S(2)}) collective-permute-start(f32[2,131072]{1,0:T(2,128)S(1)} %pad_maximum_fusion.2), channel_id=1, source_target_pairs={{0,256},{64,320},{128,384},{192,448},{256,0},{320,64},{384,128},{4... | collective-permute-start | bytes 3145736 | tf_op jit(solution)/shard_map/ppermute | solution.py:10
  235.7 4.6 %collective-permute-start.4 = (f32[2,131072]{1,0:T(2,128)S(1)}, f32[2,131072]{1,0:T(2,128)S(1)}, u32[]{:S(2)}, u32[]{:S(2)}) collective-permute-start(f32[2,131072]{1,0:T(2,128)S(1)} %pad_maximum_fusion.2), channel_id=1, source_target_pairs={{0,512},{64,576},{128,640},{192,704},{256,768},{320,832},{384,896}... | collective-permute-start | bytes 3145736 | tf_op jit(solution)/shard_map/ppermute | solution.py:10
  240.3 19.9 %collective-permute-done.3 = f32[2,131072]{1,0:T(2,128)S(1)} collective-permute-done((f32[2,131072]{1,0:T(2,128)S(1)}, f32[2,131072]{1,0:T(2,128)S(1)}, u32[]{:S(2)}, u32[]{:S(2)}) %collective-permute-start.3) | collective-permute-done | bytes 1048608 | tf_op jit(solution)/shard_map/ppermute | solution.py:10
  260.2 4.9 %collective-permute-start.5 = (f32[2,131072]{1,0:T(2,128)S(1)}, f32[2,131072]{1,0:T(2,128)S(1)}, u32[]{:S(2)}, u32[]{:S(2)}) collective-permute-start(f32[2,131072]{1,0:T(2,128)S(1)} %collective-permute-done.3), channel_id=1, source_target_pairs={{0,512},{64,576},{128,640},{192,704},{256,768},{320,832},{384,896}... | collective-permute-start | bytes 3145736 | tf_op jit(solution)/shard_map/ppermute | solution.py:10
  265.7 0.7 fusion.53
  267.0 0.6 fusion.51
  267.6 17.3 %collective-permute-done.4 = f32[2,131072]{1,0:T(2,128)S(1)} collective-permute-done((f32[2,131072]{1,0:T(2,128)S(1)}, f32[2,131072]{1,0:T(2,128)S(1)}, u32[]{:S(2)}, u32[]{:S(2)}) %collective-permute-start.4) | collective-permute-done | bytes 1048608 | tf_op jit(solution)/shard_map/ppermute | solution.py:10
  284.9 21.1 %collective-permute-done.5 = f32[2,131072]{1,0:T(2,128)S(1)} collective-permute-done((f32[2,131072]{1,0:T(2,128)S(1)}, f32[2,131072]{1,0:T(2,128)S(1)}, u32[]{:S(2)}, u32[]{:S(2)}) %collective-permute-start.5) | collective-permute-done | bytes 1048608 | tf_op jit(solution)/shard_map/ppermute | solution.py:10
  306.0 7.9 %multiply_subtract_fusion = f32[1,131072]{1,0:T(1,128)S(1)} fusion(f32[1,131072]{1,0:T(1,128)S(1)} %multiply_add_fusion.1, f32[1,131072]{1,0:T(1,128)S(1)} %multiply_subtract_fusion.1, f32[2,131072]{1,0:T(2,128)S(1)} %collective-permute-done.5, f32[2,131072]{1,0:T(2,128)S(1)} %collective-permute-done.4, f32[2,131072]{1,0:T(2,128)S(1)} %collective-permute-done.3, ...), kind=kLoop, calls=%fused_computation.17 | loop fusion | flops 1966080 | bytes 4718624 | tf_op jit(solution)/shard_map/sub | solution.py:60
  313.9 7.9 %multiply_add_fusion = f32[1,131072]{1,0:T(1,128)S(1)} fusion(f32[1,131072]{1,0:T(1,128)S(1)} %multiply_subtract_fusion.1, f32[1,131072]{1,0:T(1,128)S(1)} %multiply_add_fusion.1, f32[2,131072]{1,0:T(2,128)S(1)} %collective-permute-done.5, f32[2,131072]{1,0:T(2,128)S(1)} %collective-permute-done.4, f32[2,131072]{1,0:T(2,128)S(1)} %collective-permute-done.3, ...), kind=kLoop, calls=%fused_computation.16 | loop fusion | flops 1966080 | bytes 4718624 | tf_op jit(solution)/shard_map/add | solution.py:61
  321.8 1.9 pad_maximum_fusion.3
  (36 shorter events, 10.7 us)
Async XLA Ops:
  4.5 1.0 copy-start
  162.1 5.2 %collective-permute-start = (f32[2,131072]{1,0:T(2,128)S(1)}, f32[2,131072]{1,0:T(2,128)S(1)}, u32[]{:S(2)}, u32[]{:S(2)}) collective-permute-start(f32[2,131072]{1,0:T(2,128)S(1)} %pad_maximum_fusion.1), channel_id=1, source_target_pairs={{0,64},{64,0},{128,192},{192,128},{256,320},{320,256},{384,448},{4... | collective-permute-start | bytes 3145736 | tf_op jit(solution)/shard_map/ppermute | solution.py:10
  164.1 29.4 %collective-permute-start.1 = (f32[2,131072]{1,0:T(2,128)S(1)}, f32[2,131072]{1,0:T(2,128)S(1)}, u32[]{:S(2)}, u32[]{:S(2)}) collective-permute-start(f32[2,131072]{1,0:T(2,128)S(1)} %pad_maximum_fusion.1), channel_id=1, source_target_pairs={{0,128},{64,192},{128,0},{192,64},{256,384},{320,448},{384,256},{4... | collective-permute-start | bytes 3145736 | tf_op jit(solution)/shard_map/ppermute | solution.py:10
  167.3 48.3 %collective-permute-start.2 = (f32[2,131072]{1,0:T(2,128)S(1)}, f32[2,131072]{1,0:T(2,128)S(1)}, u32[]{:S(2)}, u32[]{:S(2)}) collective-permute-start(f32[2,131072]{1,0:T(2,128)S(1)} %collective-permute-done), channel_id=1, source_target_pairs={{0,128},{64,192},{128,0},{192,64},{256,384},{320,448},{384,256},{4... | collective-permute-start | bytes 3145736 | tf_op jit(solution)/shard_map/ppermute | solution.py:10
  171.9 0.7 copy-start.1
  232.3 27.9 %collective-permute-start.3 = (f32[2,131072]{1,0:T(2,128)S(1)}, f32[2,131072]{1,0:T(2,128)S(1)}, u32[]{:S(2)}, u32[]{:S(2)}) collective-permute-start(f32[2,131072]{1,0:T(2,128)S(1)} %pad_maximum_fusion.2), channel_id=1, source_target_pairs={{0,256},{64,320},{128,384},{192,448},{256,0},{320,64},{384,128},{4... | collective-permute-start | bytes 3145736 | tf_op jit(solution)/shard_map/ppermute | solution.py:10
  235.7 49.2 %collective-permute-start.4 = (f32[2,131072]{1,0:T(2,128)S(1)}, f32[2,131072]{1,0:T(2,128)S(1)}, u32[]{:S(2)}, u32[]{:S(2)}) collective-permute-start(f32[2,131072]{1,0:T(2,128)S(1)} %pad_maximum_fusion.2), channel_id=1, source_target_pairs={{0,512},{64,576},{128,640},{192,704},{256,768},{320,832},{384,896}... | collective-permute-start | bytes 3145736 | tf_op jit(solution)/shard_map/ppermute | solution.py:10
  260.2 45.8 %collective-permute-start.5 = (f32[2,131072]{1,0:T(2,128)S(1)}, f32[2,131072]{1,0:T(2,128)S(1)}, u32[]{:S(2)}, u32[]{:S(2)}) collective-permute-start(f32[2,131072]{1,0:T(2,128)S(1)} %collective-permute-done.3), channel_id=1, source_target_pairs={{0,512},{64,576},{128,640},{192,704},{256,768},{320,832},{384,896}... | collective-permute-start | bytes 3145736 | tf_op jit(solution)/shard_map/ppermute | solution.py:10
where the time goes:
time: 324 us
  blocking collectives  140 us (43%)
  waiting for transfers between devices  98.7 us (30%)
  other arithmetic  36.5 us (11%)
  starting transfers between devices  22.5 us (7%)
  local copies, waits for them, and re-layouts  14.8 us (5%)
  matrix products  10.9 us (3%)
    all_to_all x1, blocking collectives, on_device(): lax.all_to_all(blocks, 'qb', split_axis=1, concat_axis=1, tiled=True)  140 us
    ppermute x6, waiting for transfers between devices, from_partner(): return lax.ppermute(value, axis, pairs)  98.7 us
    ppermute x6, starting transfers between devices, from_partner(): return lax.ppermute(value, axis, pairs)  22.5 us
    add x2, other arithmetic, pair_gate(): imag_total = imag_total + weight[0] * source[1] + weight[1] * source[0]  15.8 us
    sub x2, other arithmetic, pair_gate(): real_total = real_total + weight[0] * source[0] - weight[1] * source[1]  15.7 us
    dot_general x16, matrix products, product(): lax.dot_general(left, right, numbers, precision=lax.Precision.HIGHEST, pr...  10.9 us
    slice x2, local copies, waits for them, and re-layouts, dot_parts(): real_part = product(first[0], second[0]) - product(first[1], second[1])  7.17 us
  transfers between devices with their start and end apart: 6, of which 5 were waited for; matrix products, arithmetic and copies ran while one was open for 2% of the time, Pallas kernels for 0%

commit v1 on v0

v1 whole, which is shorter than its diff:
```python
import functools

import jax
import jax.numpy as jnp
from jax import lax
from jax.experimental import pallas as pl
from jax.experimental.pallas import tpu as pltpu
from jax.sharding import PartitionSpec as P

MESH = pl.DeviceIdType.MESH
GATE = 128
NZ = 32
PARTS = 3
MIX_AT = 2
TURN_AT = (4, 5)
LATE_FROM = 7
BACK_AT = (17, 18)
BACK_MIX_AT = 21
HIGHEST = lax.Precision.HIGHEST


def ranges(low, high, parts):
    count = high - low + 1
    parts = min(parts, count)
    edges = [low + count * i // parts for i in range(parts + 1)]
    return [(edges[i], edges[i + 1] - 1) for i in reversed(range(parts))]


def kernel(groups, x_hbm, gates_hbm, cross, out_ref, first_x, late_x, gates, rep, turn,
           first_pre, late_pre, first_recv, late_recv, first_post, late_post, first_res, late_mixed, first_out, late_out,
           mix_in, mix_out, ssem, rsem, mix_s, mix_r, local_sem):
    g = lax.axis_index("grp")
    q = lax.axis_index("qb")
    z, y = q // 2, q % 2
    up, down = lax.rem(z + 1, NZ), lax.rem(z + NZ - 1, NZ)
    near = (up, down)

    barrier = pltpu.get_barrier_semaphore()

    def greet(to_g, to_q):
        pl.semaphore_signal(barrier, inc=1, device_id=(to_g, to_q), device_id_type=MESH)

    for zz in near:
        for yy in (0, 1):
            greet(g, zz * 2 + yy)
    greet(g, z * 2 + 1 - y)

    def greet_group(i, c):
        greet(lax.rem(g + i, groups), q)
        return c

    lax.fori_loop(1, groups, greet_group, 0)

    load_gates = pltpu.make_async_copy(gates_hbm, gates, local_sem.at[0])
    load_first = pltpu.make_async_copy(x_hbm.at[:, pl.ds(0, 8), :], first_x, local_sem.at[1])
    load_late = pltpu.make_async_copy(x_hbm.at[:, pl.ds(8, 8), :], late_x, local_sem.at[2])
    load_gates.start()
    load_first.start()
    load_late.start()

    def real_form(index, place):
        re, im = gates[index, 0], gates[index, 1]
        rep[place, 0:GATE, 0:GATE] = re
        rep[place, 0:GATE, GATE:] = -im
        rep[place, GATE:, 0:GATE] = im
        rep[place, GATE:, GATE:] = re

    def rows(ref, r, part):
        return ref[pl.ds(r * 2 + part, GATE, stride=8), :]

    def high_gate(place, columns):
        return jnp.dot(rep[place], columns, precision=HIGHEST, preferred_element_type=jnp.float32)

    def low_gate(stacked):
        return lax.dot_general(stacked, turn[...], (((1,), (1,)), ((), ())), precision=HIGHEST,
                               preferred_element_type=jnp.float32)

    def columns_of(ref, pair):
        return jnp.concatenate(
            [jnp.concatenate([rows(ref, r, part) for r in pair], axis=1) for part in (0, 1)], axis=0)

    def put(ref, base, pair, value):
        for i, r in enumerate(pair):
            for part in (0, 1):
                ref[pl.ds(base + r * 2 + part, GATE, stride=8), :] = value[
                    part * GATE:(part + 1) * GATE, i * GATE:(i + 1) * GATE]

    flat = (1024, GATE)
    pairs = ((0, 1), (2, 3))

    sems = {}

    def sem_of(key):
        return sems.setdefault(key, len(sems))

    sent = []

    def send(key, src, dst, to_g, to_q):
        k = sem_of(key)
        copy = pltpu.make_async_remote_copy(src_ref=src, dst_ref=dst, send_sem=ssem.at[k], recv_sem=rsem.at[k],
                                            device_id=(to_g, to_q), device_id_type=MESH)
        copy.start()
        sent.append(copy)

    def arrived(key, src, dst):
        k = sem_of(key)
        pltpu.make_async_remote_copy(src_ref=src, dst_ref=dst, send_sem=ssem.at[k], recv_sem=rsem.at[k],
                                     device_id=(g, q), device_id_type=MESH).wait_recv()

    first_n = (16, 15)

    def first_start(way, low, high):
        return low if way == 0 else 15 - high

    def first_own(way, low, high, cross_y):
        n = high - low + 1
        to_y = 1 - y if cross_y else y
        at = z + low + 1 if way == 0 else z + NZ - high - 1
        send(("f", way, 1, low, cross_y), first_pre.at[pl.ds(at, n), to_y],
             first_recv.at[way, 0, pl.ds(first_start(way, low, high), n), y], g, near[way] * 2 + to_y)

    def first_pass(way, step, low, high):
        n = high - low + 1
        send(("f", way, step, low, 0), first_recv.at[way, step - 2, pl.ds(first_start(way, low + 1, high + 1), n)],
             first_recv.at[way, step - 1, pl.ds(first_start(way, low, high), n)], g, near[way] * 2 + y)

    def first_ranges(way, step):
        return ranges(0, first_n[way] - step, PARTS) if step <= first_n[way] else []

    first_seen = set()

    def first_wait(way, step, low, high):
        if (way, step, low) in first_seen:
            return
        first_seen.add((way, step, low))
        n = high - low + 1
        at = first_start(way, low, high)
        if step == 1:
            for cross_y in (0, 1):
                from_y = 1 - y if cross_y else y
                arrived(("f", way, 1, low, cross_y), first_pre.at[pl.ds(0, n), 0],
                        first_recv.at[way, 0, pl.ds(at, n), from_y])
        else:
            ref = first_recv.at[way, step - 1, pl.ds(at, n)]
            arrived(("f", way, step, low, 0), ref, ref)

    def keep(post, z_from, block):
        post[pl.ds(pl.multiple_of(z_from * 32, 32), 32), :] = block.reshape(32, GATE)

    def first_step(step):
        for index in range(PARTS):
            for way in (0, 1):
                onward = first_ranges(way, step + 1)
                if index < len(onward):
                    low, high = onward[index]
                    for a, b in first_ranges(way, step):
                        if a <= high + 1 and b >= low + 1:
                            first_wait(way, step, a, b)
                    first_pass(way, step + 1, low, high)
        for way in (0, 1):
            if step <= first_n[way]:
                for a, b in first_ranges(way, step):
                    first_wait(way, step, a, b)
                z_from = lax.rem(z + NZ - step, NZ) if way == 0 else lax.rem(z + step, NZ)
                keep(first_post, z_from, first_recv[way, step - 1, first_start(way, 0, 0)])

    late_n = (15, 16)

    def late_own(way, phase, cross_y):
        left = late_n[way] - phase + 1
        to_y = 1 - y if cross_y else y
        at = z + left if way == 0 else z + NZ - left
        send(("l", way, phase, 0, cross_y), late_pre.at[at, to_y], late_recv.at[way, phase - 1, 0, y],
             g, near[way] * 2 + to_y)

    def late_pass(way, phase, low, high):
        n = high - low + 1
        send(("l", way, phase, low, 0), late_recv.at[way, phase - 2, pl.ds(low - 1, n)],
             late_recv.at[way, phase - 1, pl.ds(low, n)], g, near[way] * 2 + y)

    def late_ranges(phase):
        return list(reversed(ranges(1, phase - 1, PARTS))) if phase > 1 else []

    late_seen = set()

    def late_wait(way, phase, low, high):
        if (way, phase, low) in late_seen:
            return
        late_seen.add((way, phase, low))
        if low == 0:
            for cross_y in (0, 1):
                from_y = 1 - y if cross_y else y
                arrived(("l", way, phase, 0, cross_y), late_pre.at[0, 0], late_recv.at[way, phase - 1, 0, from_y])
        else:
            ref = late_recv.at[way, phase - 1, pl.ds(low, high - low + 1)]
            arrived(("l", way, phase, low, 0), ref, ref)

    def late_parts(phase):
        return [(0, 0)] + late_ranges(phase)

    def late_phase(phase):
        for way in (0, 1):
            if phase <= late_n[way]:
                for cross_y in (1, 0):
                    late_own(way, phase, cross_y)
        for index, (low, high) in enumerate(late_ranges(phase)):
            for way in (0, 1):
                if phase <= late_n[way]:
                    for a, b in late_parts(phase - 1):
                        if a <= high - 1 and b >= low - 1:
                            late_wait(way, phase - 1, a, b)
                    late_pass(way, phase, low, high)

    def beside(key, pre, post):
        send((key, "beside"), pre.at[z, 1 - y], post.at[pl.ds(pl.multiple_of((z * 2 + y) * 16, 16), 16)],
             g, z * 2 + 1 - y)
        post[pl.ds(pl.multiple_of((z * 2 + y) * 16, 16), 16), :] = pre[z, y]

    def beside_wait(key, pre, post):
        arrived((key, "beside"), pre.at[0, 0], post.at[pl.ds(pl.multiple_of((z * 2 + 1 - y) * 16, 16), 16)])

    def mix_send(which, source):
        def body(i, c):
            j = lax.rem(g + i, groups)
            pltpu.make_async_remote_copy(
                src_ref=source.at[pl.ds(j * 8, 8)], dst_ref=mix_in.at[which, g], send_sem=mix_s.at[which, 0, i],
                recv_sem=mix_r.at[which, 0, i], device_id=(j, q), device_id_type=MESH).start()
            return c
        lax.fori_loop(1, groups, body, 0)
        mix_in[which, g] = source[pl.ds(g * 8, 8)]

    def mix(which, target):
        def wait(i, c):
            j = lax.rem(g + groups - i, groups)
            pltpu.make_async_remote_copy(
                src_ref=target.at[pl.ds(0, 8)], dst_ref=mix_in.at[which, j], send_sem=mix_s.at[which, 0, i],
                recv_sem=mix_r.at[which, 0, i], device_id=(j, q), device_id_type=MESH).wait_recv()
            return c
        lax.fori_loop(1, groups, wait, 0)
        taken = mix_in.reshape(2 * 16 * 64, GATE)
        given = mix_out.reshape(2 * 16 * 64, GATE)
        low = [[(cross[0, 0, i, j], cross[0, 1, i, j]) for j in range(4)] for i in range(4)]
        high = [[(cross[1, 0, i, j], cross[1, 1, i, j]) for j in range(4)] for i in range(4)]

        def combine(matrix, vectors):
            out = []
            for i in range(4):
                re = im = None
                for j in range(4):
                    (cr, ci), (vr, vi) = matrix[i][j], vectors[j]
                    tr, ti = cr * vr - ci * vi, cr * vi + ci * vr
                    re, im = (tr, ti) if re is None else (re + tr, im + ti)
                out.append((re, im))
            return out

        def piece(n, c):
            def at(a, part):
                return pl.ds((which * 16 + a) * 64 + n * 16 + part, 8, stride=2)
            five = []
            for hi in range(4):
                five.append(combine(low, [(taken[at(hi * 4 + lo, 0), :], taken[at(hi * 4 + lo, 1), :])
                                          for lo in range(4)]))
            for lo in range(4):
                for hi, (re, im) in enumerate(combine(high, [five[h][lo] for h in range(4)])):
                    given[at(hi * 4 + lo, 0), :] = re
                    given[at(hi * 4 + lo, 1), :] = im
            return c
        lax.fori_loop(0, 4, piece, 0)

        def body(i, c):
            j = lax.rem(g + i, groups)
            pltpu.make_async_remote_copy(
                src_ref=mix_out.at[which, j], dst_ref=target.at[pl.ds(g * 8, 8)], send_sem=mix_s.at[which, 1, i],
                recv_sem=mix_r.at[which, 1, i], device_id=(j, q), device_id_type=MESH).start()
            return c
        lax.fori_loop(1, groups, body, 0)
        target[pl.ds(g * 8, 8)] = mix_out[which, g]

    def mix_wait(which, target):
        def wait(i, c):
            j = lax.rem(g + groups - i, groups)
            pltpu.make_async_remote_copy(
                src_ref=mix_out.at[which, 0], dst_ref=target.at[pl.ds(j * 8, 8)], send_sem=mix_s.at[which, 1, i],
                recv_sem=mix_r.at[which, 1, i], device_id=(j, q), device_id_type=MESH).wait_recv()
            return c
        lax.fori_loop(1, groups, wait, 0)

    def mix_done(which, target):
        def wait(i, c):
            for half in (0, 1):
                pltpu.make_async_remote_copy(
                    src_ref=mix_out.at[which, 0], dst_ref=mix_in.at[which, 0], send_sem=mix_s.at[which, half, i],
                    recv_sem=mix_r.at[which, half, i], device_id=(g, q), device_id_type=MESH).wait_send()
            return c
        lax.fori_loop(1, groups, wait, 0)

    load_gates.wait()
    real_form(0, 0)
    load_first.wait()
    for pair in pairs:
        value = high_gate(0, columns_of(first_x.reshape(*flat), pair))
        for base in (0, 1024):
            put(first_pre.reshape(2048, GATE), base, pair, value)
    pl.semaphore_wait(barrier, groups - 1 + 5)
    for index in range(PARTS):
        for cross_y in (1, 0):
            for way in (0, 1):
                first_own(way, *first_ranges(way, 1)[index], cross_y)
    load_late.wait()
    mix_send(0, late_x)
    beside("f", first_pre, first_post)
    real_form(1, 1)
    real_form(3, 2)
    turn[...] = jnp.dot(rep[2], rep[1], precision=HIGHEST, preferred_element_type=jnp.float32)
    real_form(2, 1)

    def late_before(pair):
        source = late_mixed.reshape(*flat)
        stacked = jnp.concatenate(
            [jnp.concatenate([rows(source, r, part) for part in (0, 1)], axis=1) for r in pair], axis=0)
        turned = low_gate(stacked)
        columns = jnp.concatenate(
            [jnp.concatenate([turned[i * GATE:(i + 1) * GATE, part * GATE:(part + 1) * GATE] for i in (0, 1)], axis=1)
             for part in (0, 1)], axis=0)
        value = high_gate(0, columns)
        for base in (0, 1024):
            put(late_pre.reshape(2048, GATE), base, pair, value)

    def first_after(pair):
        value = high_gate(1, columns_of(first_post, pair))
        stacked = jnp.concatenate(
            [jnp.concatenate([value[part * GATE:(part + 1) * GATE, i * GATE:(i + 1) * GATE] for part in (0, 1)], axis=1)
             for i in (0, 1)], axis=0)
        turned = low_gate(stacked)
        result = first_res.reshape(*flat)
        for i, r in enumerate(pair):
            for part in (0, 1):
                result[pl.ds(r * 2 + part, GATE, stride=8), :] = turned[
                    i * GATE:(i + 1) * GATE, part * GATE:(part + 1) * GATE]

    last = LATE_FROM + 16
    for tick in range(1, last + 1):
        if tick <= 16:
            first_step(tick)
        if tick > LATE_FROM:
            late_phase(tick - LATE_FROM)
        if tick == MIX_AT:
            mix(0, late_mixed)
        for i in (0, 1):
            if tick == TURN_AT[i]:
                if i == 0:
                    mix_wait(0, late_mixed)
                late_before(pairs[i])
        if tick == LATE_FROM:
            beside("l", late_pre, late_post)
        for i in (0, 1):
            if tick == BACK_AT[i]:
                if i == 0:
                    beside_wait("f", first_pre, first_post)
                first_after(pairs[i])
                if i == 1:
                    mix_send(1, first_res)
        if tick == BACK_MIX_AT:
            mix(1, first_out)

    mix_wait(1, first_out)
    store_first = pltpu.make_async_copy(first_out, out_ref.at[:, pl.ds(0, 8), :], local_sem.at[3])
    store_first.start()

    beside_wait("l", late_pre, late_post)
    for way in (0, 1):
        n = late_n[way]
        for a, b in late_parts(n):
            late_wait(way, n, a, b)
        for k in range(n):
            z_from = lax.rem(z + NZ - k - 1, NZ) if way == 0 else lax.rem(z + k + 1, NZ)
            keep(late_post, z_from, late_recv[way, n - 1, k])
    for pair in pairs:
        put(late_out.reshape(*flat), 0, pair, high_gate(1, columns_of(late_post, pair)))
    store_late = pltpu.make_async_copy(late_out, out_ref.at[:, pl.ds(8, 8), :], local_sem.at[4])
    store_late.start()

    for copy in sent:
        copy.wait_send()
    mix_done(0, late_mixed)
    mix_done(1, first_out)
    store_first.wait()
    store_late.wait()


def on_device(amplitudes, layer_gates, cross_gates):
    groups = lax.axis_size("grp")
    view = amplitudes.reshape(2, 1024, GATE).transpose(1, 0, 2).reshape(GATE, 16, GATE)
    vm = lambda *shape: pltpu.VMEM(shape, jnp.float32)
    result = pl.pallas_call(
        functools.partial(kernel, groups),
        out_shape=jax.ShapeDtypeStruct((GATE, 16, GATE), jnp.float32),
        in_specs=[pl.BlockSpec(memory_space=pl.ANY), pl.BlockSpec(memory_space=pl.ANY),
                  pl.BlockSpec(memory_space=pltpu.SMEM)],
        out_specs=pl.BlockSpec(memory_space=pl.ANY),
        scratch_shapes=[
            vm(GATE, 8, GATE), vm(GATE, 8, GATE), vm(4, 2, GATE, GATE), vm(3, 256, 256), vm(256, 256),
            vm(64, 2, 16, GATE), vm(64, 2, 16, GATE), vm(2, 16, 16, 2, 16, GATE), vm(2, 16, 16, 2, 16, GATE),
            vm(1024, GATE), vm(1024, GATE), vm(GATE, 8, GATE), vm(GATE, 8, GATE), vm(GATE, 8, GATE), vm(GATE, 8, GATE),
            vm(2, 16, 8, 8, GATE), vm(2, 16, 8, 8, GATE),
            pltpu.SemaphoreType.DMA((272,)), pltpu.SemaphoreType.DMA((272,)),
            pltpu.SemaphoreType.DMA((2, 2, 16)), pltpu.SemaphoreType.DMA((2, 2, 16)),
            pltpu.SemaphoreType.DMA((5,)),
        ],
        compiler_params=pltpu.CompilerParams(collective_id=0, has_side_effects=True,
                                             vmem_limit_bytes=60 * 1024 * 1024),
    )(view, layer_gates, cross_gates)
    return result.reshape(1024, 2, GATE).transpose(1, 0, 2).reshape(2, -1)


def solution(mesh):
    return jax.shard_map(
        on_device,
        mesh=mesh,
        in_specs=(P(None, ("grp", "qb")), P(), P()),
        out_specs=P(None, ("grp", "qb")),
        check_vma=False,
    )
```

time: 324 us -> 135 us (0.42)
  blocking collectives: 140 us -> 0 us
  Pallas kernels: 0 us -> 132 us
  waiting for transfers between devices: 98.7 us -> 0 us
  other arithmetic: 36.5 us -> 0 us
  starting transfers between devices: 22.5 us -> 0 us
  local copies, waits for them, and re-layouts: 14.8 us -> 2.26 us
  matrix products: 10.9 us -> 0 us
    all_to_all x1 -> x0, blocking collectives: 140 us -> none  [on_device(): lax.all_to_all(blocks, 'qb', split_axis=1, concat_axis=1, tiled=True)]
    pallas_call x0 -> x1, Pallas kernels: none -> 132 us  [on_device(): pl.pallas_call(functools.partial(kernel, groups), out_shape=jax.ShapeDtyp...]
    ppermute x6 -> x0, waiting for transfers between devices: 98.7 us -> none  [from_partner(): return lax.ppermute(value, axis, pairs)]
    ppermute x6 -> x0, starting transfers between devices: 22.5 us -> none  [from_partner(): return lax.ppermute(value, axis, pairs)]
    add x2 -> x0, other arithmetic: 15.8 us -> none  [pair_gate(): imag_total = imag_total + weight[0] * source[1] + weight[1] * source[0]]
    sub x2 -> x0, other arithmetic: 15.7 us -> none  [pair_gate(): real_total = real_total + weight[0] * source[0] - weight[1] * source[1]]
    slice x10 -> x0, local copies, waits for them, and re-layouts: 12.1 us -> none  [the longest x2 7.17 us: dot_parts(): real_part = product(first[0], second[0]) - product(first[1], second[1])]
    dot_general x16 -> x0, matrix products: 10.9 us -> none  [product(): lax.dot_general(left, right, numbers, precision=lax.Precision.HIGHEST, pr...]
  transfers between devices with their start and end apart: 6 -> 0, of which waited for: 5 -> 0; matrix products, arithmetic and copies ran while one was open for 2% -> 0% of each run, Pallas kernels for 0% -> 0%
where the time goes in v1:
time: 135 us; the launch traced here: 134 us
  Pallas kernels  132 us (98%)
  local copies, waits for them, and re-layouts  2.26 us (2%)
    pallas_call x1, Pallas kernels, on_device(): pl.pallas_call(functools.partial(kernel, groups), out_shape=jax.ShapeDtyp...  132 us

profile of v1, /device:TPU:24, one launch (start us, length us, event | category | flops | bytes accessed | tf_op | source)
XLA Modules:
  0.0 134.2 jit_solution(13132243491575481911)
XLA Ops:
  0.0 131.9 %shard_map.37 = f32[128,16,128]{2,1,0:T(8,128)} custom-call(f32[128,16,128]{2,1,0:T(8,128)} %bitcast.11, f32[4,2,128,128]{3,2,1,0:T(8,128)} %gates_hbm.1, f32[2,2,4,4]{3,2,1,0:T(4,128)} %cross.1), custom_call_target="tpu_custom_call" | custom-call | tf_op jit(solution)/shard_map/pallas_call | solution.py:395
  131.9 2.3 %copy.7 = f32[2,131072]{1,0:T(2,128)} copy(f32[2,131072]{1,0:T(2,128)} %bitcast.10) | data formatting | bytes 2097152

commit v2 on v1

--- a/solution.py
+++ b/solution.py
@@ -10,12 +10,13 @@
 MESH = pl.DeviceIdType.MESH
 GATE = 128
 NZ = 32
-PARTS = 3
+PARTS = 4
 MIX_AT = 2
 TURN_AT = (4, 5)
 LATE_FROM = 7
 BACK_AT = (17, 18)
 BACK_MIX_AT = 21
+MESSAGES = 257
 HIGHEST = lax.Precision.HIGHEST
 
 
@@ -27,7 +28,7 @@
 
 
 def kernel(groups, x_hbm, gates_hbm, cross, out_ref, first_x, late_x, gates, rep, turn,
-           first_pre, late_pre, first_recv, late_recv, first_post, late_post, first_res, late_mixed, first_out, late_out,
+           first_pre, late_pre, late_src, first_recv, late_recv, first_post, late_post, first_res, late_mixed, first_out, late_out,
            mix_in, mix_out, ssem, rsem, mix_s, mix_r, local_sem):
     g = lax.axis_index("grp")
     q = lax.axis_index("qb")
@@ -51,12 +52,14 @@
 
     lax.fori_loop(1, groups, greet_group, 0)
 
-    load_gates = pltpu.make_async_copy(gates_hbm, gates, local_sem.at[0])
+    load_gates = [pltpu.make_async_copy(gates_hbm.at[i], gates.at[i], local_sem.at[5 + i]) for i in range(4)]
     load_first = pltpu.make_async_copy(x_hbm.at[:, pl.ds(0, 8), :], first_x, local_sem.at[1])
     load_late = pltpu.make_async_copy(x_hbm.at[:, pl.ds(8, 8), :], late_x, local_sem.at[2])
-    load_gates.start()
     load_first.start()
+    load_gates[0].start()
     load_late.start()
+    for i in (1, 3, 2):
+        load_gates[i].start()
 
     def real_form(index, place):
         re, im = gates[index, 0], gates[index, 1]
@@ -93,18 +96,19 @@
     def sem_of(key):
         return sems.setdefault(key, len(sems))
 
-    sent = []
+    kinds = ("f", "l", "fy", "ly")
 
     def send(key, src, dst, to_g, to_q):
-        k = sem_of(key)
-        copy = pltpu.make_async_remote_copy(src_ref=src, dst_ref=dst, send_sem=ssem.at[k], recv_sem=rsem.at[k],
-                                            device_id=(to_g, to_q), device_id_type=MESH)
-        copy.start()
-        sent.append(copy)
+        pltpu.make_async_remote_copy(src_ref=src, dst_ref=dst, send_sem=ssem.at[kinds.index(key[0])],
+                                     recv_sem=rsem.at[sem_of(key)], device_id=(to_g, to_q),
+                                     device_id_type=MESH).start()
+
+    def sent(kind, like):
+        pltpu.make_async_remote_copy(src_ref=like, dst_ref=like, send_sem=ssem.at[kinds.index(kind)],
+                                     recv_sem=rsem.at[0], device_id=(g, q), device_id_type=MESH).wait_send()
 
     def arrived(key, src, dst):
-        k = sem_of(key)
-        pltpu.make_async_remote_copy(src_ref=src, dst_ref=dst, send_sem=ssem.at[k], recv_sem=rsem.at[k],
+        pltpu.make_async_remote_copy(src_ref=src, dst_ref=dst, send_sem=ssem.at[0], recv_sem=rsem.at[sem_of(key)],
                                      device_id=(g, q), device_id_type=MESH).wait_recv()
 
     first_n = (16, 15)
@@ -166,16 +170,14 @@
 
     late_n = (15, 16)
 
-    def late_own(way, phase, cross_y):
+    def late_own(way, phase):
         left = late_n[way] - phase + 1
-        to_y = 1 - y if cross_y else y
-        at = z + left if way == 0 else z + NZ - left
-        send(("l", way, phase, 0, cross_y), late_pre.at[at, to_y], late_recv.at[way, phase - 1, 0, y],
-             g, near[way] * 2 + to_y)
+        at = lax.rem(z + left, NZ) if way == 0 else lax.rem(z + NZ - left, NZ)
+        send(("l", way, phase, 0), late_src.at[at], late_recv.at[way, phase - 1, 0], g, near[way] * 2 + y)
 
     def late_pass(way, phase, low, high):
         n = high - low + 1
-        send(("l", way, phase, low, 0), late_recv.at[way, phase - 2, pl.ds(low - 1, n)],
+        send(("l", way, phase, low), late_recv.at[way, phase - 2, pl.ds(low - 1, n)],
              late_recv.at[way, phase - 1, pl.ds(low, n)], g, near[way] * 2 + y)
 
     def late_ranges(phase):
@@ -187,13 +189,8 @@
         if (way, phase, low) in late_seen:
             return
         late_seen.add((way, phase, low))
-        if low == 0:
-            for cross_y in (0, 1):
-                from_y = 1 - y if cross_y else y
-                arrived(("l", way, phase, 0, cross_y), late_pre.at[0, 0], late_recv.at[way, phase - 1, 0, from_y])
-        else:
-            ref = late_recv.at[way, phase - 1, pl.ds(low, high - low + 1)]
-            arrived(("l", way, phase, low, 0), ref, ref)
+        ref = late_recv.at[way, phase - 1, pl.ds(low, high - low + 1)]
+        arrived(("l", way, phase, low), ref, ref)
 
     def late_parts(phase):
         return [(0, 0)] + late_ranges(phase)
@@ -201,8 +198,7 @@
     def late_phase(phase):
         for way in (0, 1):
             if phase <= late_n[way]:
-                for cross_y in (1, 0):
-                    late_own(way, phase, cross_y)
+                late_own(way, phase)
         for index, (low, high) in enumerate(late_ranges(phase)):
             for way in (0, 1):
                 if phase <= late_n[way]:
@@ -211,32 +207,46 @@
                             late_wait(way, phase - 1, a, b)
                     late_pass(way, phase, low, high)
 
-    def beside(key, pre, post):
-        send((key, "beside"), pre.at[z, 1 - y], post.at[pl.ds(pl.multiple_of((z * 2 + y) * 16, 16), 16)],
+    def first_beside():
+        send(("fy",), first_pre.at[z, 1 - y], first_post.at[pl.ds(pl.multiple_of((z * 2 + y) * 16, 16), 16)],
              g, z * 2 + 1 - y)
-        post[pl.ds(pl.multiple_of((z * 2 + y) * 16, 16), 16), :] = pre[z, y]
-
-    def beside_wait(key, pre, post):
-        arrived((key, "beside"), pre.at[0, 0], post.at[pl.ds(pl.multiple_of((z * 2 + 1 - y) * 16, 16), 16)])
+        first_post[pl.ds(pl.multiple_of((z * 2 + y) * 16, 16), 16), :] = first_pre[z, y]
+
+    def first_beside_wait():
+        arrived(("fy",), first_pre.at[0, 0], first_post.at[pl.ds(pl.multiple_of((z * 2 + 1 - y) * 16, 16), 16)])
+
+    def late_beside():
+        send(("ly",), late_pre.at[:, 1 - y], late_src.at[:, y], g, z * 2 + 1 - y)
+        late_src[:, y] = late_pre[:, y]
+
+    def late_beside_wait():
+        arrived(("ly",), late_pre.at[:, 0], late_src.at[:, 1 - y])
+        keep(late_post, z, late_src[z])
 
     def mix_send(which, source):
         def body(i, c):
             j = lax.rem(g + i, groups)
             pltpu.make_async_remote_copy(
-                src_ref=source.at[pl.ds(j * 8, 8)], dst_ref=mix_in.at[which, g], send_sem=mix_s.at[which, 0, i],
-                recv_sem=mix_r.at[which, 0, i], device_id=(j, q), device_id_type=MESH).start()
+                src_ref=source.at[pl.ds(j * 8, 8)], dst_ref=mix_in.at[which, g], send_sem=mix_s.at[which, 0],
+                recv_sem=mix_r.at[which, 0], device_id=(j, q), device_id_type=MESH).start()
             return c
         lax.fori_loop(1, groups, body, 0)
         mix_in[which, g] = source[pl.ds(g * 8, 8)]
 
+    def mix_copy(which, half):
+        others = mix_in.at[which, pl.ds(0, groups - 1)]
+        return pltpu.make_async_remote_copy(
+            src_ref=others, dst_ref=others, send_sem=mix_s.at[which, half], recv_sem=mix_r.at[which, half],
+            device_id=(g, q), device_id_type=MESH)
+
+    def mix_arrived(which, half):
+        mix_copy(which, half).wait_recv()
+
+    def mix_sent(which, half):
+        mix_copy(which, half).wait_send()
+
     def mix(which, target):
-        def wait(i, c):
-            j = lax.rem(g + groups - i, groups)
-            pltpu.make_async_remote_copy(
-                src_ref=target.at[pl.ds(0, 8)], dst_ref=mix_in.at[which, j], send_sem=mix_s.at[which, 0, i],
-                recv_sem=mix_r.at[which, 0, i], device_id=(j, q), device_id_type=MESH).wait_recv()
-            return c
-        lax.fori_loop(1, groups, wait, 0)
+        mix_arrived(which, 0)
         taken = mix_in.reshape(2 * 16 * 64, GATE)
         given = mix_out.reshape(2 * 16 * 64, GATE)
         low = [[(cross[0, 0, i, j], cross[0, 1, i, j]) for j in range(4)] for i in range(4)]
@@ -270,31 +280,13 @@
         def body(i, c):
             j = lax.rem(g + i, groups)
             pltpu.make_async_remote_copy(
-                src_ref=mix_out.at[which, j], dst_ref=target.at[pl.ds(g * 8, 8)], send_sem=mix_s.at[which, 1, i],
-                recv_sem=mix_r.at[which, 1, i], device_id=(j, q), device_id_type=MESH).start()
+                src_ref=mix_out.at[which, j], dst_ref=target.at[pl.ds(g * 8, 8)], send_sem=mix_s.at[which, 1],
+                recv_sem=mix_r.at[which, 1], device_id=(j, q), device_id_type=MESH).start()
             return c
         lax.fori_loop(1, groups, body, 0)
         target[pl.ds(g * 8, 8)] = mix_out[which, g]
 
-    def mix_wait(which, target):
-        def wait(i, c):
-            j = lax.rem(g + groups - i, groups)
-            pltpu.make_async_remote_copy(
-                src_ref=mix_out.at[which, 0], dst_ref=target.at[pl.ds(j * 8, 8)], send_sem=mix_s.at[which, 1, i],
-                recv_sem=mix_r.at[which, 1, i], device_id=(j, q), device_id_type=MESH).wait_recv()
-            return c
-        lax.fori_loop(1, groups, wait, 0)
-
-    def mix_done(which, target):
-        def wait(i, c):
-            for half in (0, 1):
-                pltpu.make_async_remote_copy(
-                    src_ref=mix_out.at[which, 0], dst_ref=mix_in.at[which, 0], send_sem=mix_s.at[which, half, i],
-                    recv_sem=mix_r.at[which, half, i], device_id=(g, q), device_id_type=MESH).wait_send()
-            return c
-        lax.fori_loop(1, groups, wait, 0)
-
-    load_gates.wait()
+    load_gates[0].wait()
     real_form(0, 0)
     load_first.wait()
     for pair in pairs:
@@ -308,7 +300,9 @@
                 first_own(way, *first_ranges(way, 1)[index], cross_y)
     load_late.wait()
     mix_send(0, late_x)
-    beside("f", first_pre, first_post)
+    first_beside()
+    for i in (1, 3, 2):
+        load_gates[i].wait()
     real_form(1, 1)
     real_form(3, 2)
     turn[...] = jnp.dot(rep[2], rep[1], precision=HIGHEST, preferred_element_type=jnp.float32)
@@ -322,9 +316,7 @@
         columns = jnp.concatenate(
             [jnp.concatenate([turned[i * GATE:(i + 1) * GATE, part * GATE:(part + 1) * GATE] for i in (0, 1)], axis=1)
              for part in (0, 1)], axis=0)
-        value = high_gate(0, columns)
-        for base in (0, 1024):
-            put(late_pre.reshape(2048, GATE), base, pair, value)
+        put(late_pre.reshape(*flat), 0, pair, high_gate(0, columns))
 
     def first_after(pair):
         value = high_gate(1, columns_of(first_post, pair))
@@ -349,25 +341,26 @@
         for i in (0, 1):
             if tick == TURN_AT[i]:
                 if i == 0:
-                    mix_wait(0, late_mixed)
+                    mix_arrived(0, 1)
                 late_before(pairs[i])
+        if tick == TURN_AT[1]:
+            late_beside()
         if tick == LATE_FROM:
-            beside("l", late_pre, late_post)
+            late_beside_wait()
         for i in (0, 1):
             if tick == BACK_AT[i]:
                 if i == 0:
-                    beside_wait("f", first_pre, first_post)
+                    first_beside_wait()
                 first_after(pairs[i])
                 if i == 1:
                     mix_send(1, first_res)
         if tick == BACK_MIX_AT:
             mix(1, first_out)
 
-    mix_wait(1, first_out)
+    mix_arrived(1, 1)
     store_first = pltpu.make_async_copy(first_out, out_ref.at[:, pl.ds(0, 8), :], local_sem.at[3])
     store_first.start()
 
-    beside_wait("l", late_pre, late_post)
     for way in (0, 1):
         n = late_n[way]
         for a, b in late_parts(n):
@@ -380,10 +373,14 @@
     store_late = pltpu.make_async_copy(late_out, out_ref.at[:, pl.ds(8, 8), :], local_sem.at[4])
     store_late.start()
 
-    for copy in sent:
-        copy.wait_send()
-    mix_done(0, late_mixed)
-    mix_done(1, first_out)
+    assert len(sems) <= MESSAGES, len(sems)
+    sent("f", first_recv.at[0])
+    sent("l", late_recv.at[0])
+    sent("fy", first_pre.at[0, 0])
+    sent("ly", late_pre.at[:, 0])
+    for which in (0, 1):
+        for half in (0, 1):
+            mix_sent(which, half)
     store_first.wait()
     store_late.wait()
 
@@ -400,12 +397,12 @@
         out_specs=pl.BlockSpec(memory_space=pl.ANY),
         scratch_shapes=[
             vm(GATE, 8, GATE), vm(GATE, 8, GATE), vm(4, 2, GATE, GATE), vm(3, 256, 256), vm(256, 256),
-            vm(64, 2, 16, GATE), vm(64, 2, 16, GATE), vm(2, 16, 16, 2, 16, GATE), vm(2, 16, 16, 2, 16, GATE),
+            vm(2 * NZ, 2, 16, GATE), vm(NZ, 2, 16, GATE), vm(NZ, 2, 16, GATE), vm(2, 16, 16, 2, 16, GATE), vm(2, 16, 16, 2, 16, GATE),
             vm(1024, GATE), vm(1024, GATE), vm(GATE, 8, GATE), vm(GATE, 8, GATE), vm(GATE, 8, GATE), vm(GATE, 8, GATE),
             vm(2, 16, 8, 8, GATE), vm(2, 16, 8, 8, GATE),
-            pltpu.SemaphoreType.DMA((272,)), pltpu.SemaphoreType.DMA((272,)),
-            pltpu.SemaphoreType.DMA((2, 2, 16)), pltpu.SemaphoreType.DMA((2, 2, 16)),
-            pltpu.SemaphoreType.DMA((5,)),
+            pltpu.SemaphoreType.DMA((4,)), pltpu.SemaphoreType.DMA((MESSAGES,)),
+            pltpu.SemaphoreType.DMA((2, 2)), pltpu.SemaphoreType.DMA((2, 2)),
+            pltpu.SemaphoreType.DMA((9,)),
         ],
         compiler_params=pltpu.CompilerParams(collective_id=0, has_side_effects=True,
                                              vmem_limit_bytes=60 * 1024 * 1024),

time: 135 us -> 129 us (0.956)
  Pallas kernels: 132 us -> 127 us
    pallas_call x1, Pallas kernels: 132 us -> 127 us  [on_device(): pl.pallas_call(functools.partial(kernel, groups), out_shape=jax.ShapeDtyp...]
where the time goes in v2:
time: 129 us
  Pallas kernels  127 us (98%)
  local copies, waits for them, and re-layouts  2.26 us (2%)
    pallas_call x1, Pallas kernels, on_device(): pl.pallas_call(functools.partial(kernel, groups), out_shape=jax.ShapeDtyp...  127 us

profile of v2, /device:TPU:24, one launch (start us, length us, event | category | flops | bytes accessed | tf_op | source)
XLA Modules:
  0.0 128.9 jit_solution(9907992281689111323)
XLA Ops:
  0.0 126.6 %shard_map.37 = f32[128,16,128]{2,1,0:T(8,128)} custom-call(f32[128,16,128]{2,1,0:T(8,128)} %bitcast.11, f32[4,2,128,128]{3,2,1,0:T(8,128)} %gates_hbm.1, f32[2,2,4,4]{3,2,1,0:T(4,128)} %cross.1), custom_call_target="tpu_custom_call" | custom-call | tf_op jit(solution)/shard_map/pallas_call | solution.py:392
  126.6 2.3 %copy.7 = f32[2,131072]{1,0:T(2,128)} copy(f32[2,131072]{1,0:T(2,128)} %bitcast.10) | data formatting | bytes 2097152
